TPU v7x, 256 devices: a whole 4x4x8 slice. The times are simulated.
256 devices in a mesh: space: 32 (over z_lo, y, core), dom: 8 (over z_hi, x).
Axes of the slice: x: 4, y: 4, z: 8 (z_hi: 2, z_lo: 4; z = z_hi * 4 + z_lo), core: 2. Of those that a mesh axis runs over, the one named last changes fastest.
Arguments:
- water_depth: float32 [16, 32, 256, 512], P('dom', 'space'), may hold values from 0 to 1.5
- infiltrated: float32 [16, 32, 256, 512], P('dom', 'space'), may hold values from 0.2 to 2
- terrain: float32 [32, 256, 512], P('space'), may hold values from -3 to 3
- land_mask: int32 [32, 256, 512], P('space'), may hold values from 0 to 1
- forcing: bfloat16 [2, 2, 32, 256, 512], P(None, None, 'space', 'dom'), may hold values from 0.049804688 to 1.5
- observed: bfloat16 [2, 32, 256, 512], P(None, 'space'), may hold values from 0 to 3.6
- conductivity: float32 [16], replicated, may hold values from 0.05 to 0.6
- suction: float32 [16], replicated, may hold values from 0.1 to 2
- manning: float32 [16], replicated, may hold values from 0.5 to 2
- assignment: int32 [16], P('dom'), may hold values from 0 to 15, each once
- ancestors: int32 [16], P('dom'), may hold values from 0 to 15, as said below
- prior_weight: float32 [16], P('dom'), may hold values from 0.01 to 1
Outputs:
- final_depth: float32 [16, 32, 256, 512], P('dom', 'space')
- final_infiltrated: float32 [16, 32, 256, 512], P('dom', 'space')
- weights: float32 [16], P('dom')
Inputs may be any that keep to these rules, and one draw needn't show every extreme that they name: `ancestors`: the ancestor of slot s is a slot of its own group, 2 * (s // 2) to 2 * (s // 2) + 1; slot 0's ancestor is 0 and the last slot's is itself.
All inputs are finite; a program needn't handle non-finite values.
Results may differ from a plain program's by a relative error of at most 0.0003.
Values may be sent and summed in bfloat16 or wider, within the bound.
No kernel may reach another device: no remote copies, remote signals or barrier semaphores. Data moves between devices by JAX's collectives and lax.ppermute only.
A program may use at most 64 MiB of HBM per device.

v0:
```python
import jax
import jax.numpy as jnp
from jax import lax
from jax.experimental import pallas as pl
from jax.experimental.pallas import tpu as pltpu
from jax.sharding import PartitionSpec as P


TX = 4
SUB = 6
HOURS = 2
TIME_STEP = 0.01
SLOPE_FLOOR = 0.1
SHARPNESS = 20.0

CY, CX = 256, 512
HALO = SUB * HOURS
COLS = 16
EXT = CY + 2 * HALO
LANES = 128
CHUNKS = CX // LANES
TILES = 7
WIDE = 2 * CHUNKS + 1

RAIN_SCALE = 4096.0
WATER_SCALE = 20000.0
SOAK_SCALE = 16000.0
GROUND_SCALE = 10000.0

FIELDS = 8
ROW_FIELDS = 6
ROW_BLOCK = 80
SHARD = 32
WATER_BODY = -1e30
SCALES = (WATER_SCALE, WATER_SCALE, SOAK_SCALE, SOAK_SCALE, GROUND_SCALE, 1.0, RAIN_SCALE, RAIN_SCALE)
FROM_EAST = (4, 0, 5, 1, 2, 6, 3, 7)
FROM_WEST = (3, 7, 2, 6, 1, 5, 0, 4)


def lane_ids(rows):
    return lax.broadcasted_iota(jnp.int32, (rows, LANES), 1)


def coded(value, scale):
    scaled = value * scale
    return (scaled + jnp.where(scaled >= 0, 0.5, -0.5)).astype(jnp.int32)


def rolled(value, shift, axis=1):
    shift = shift % value.shape[axis]
    return value if shift == 0 else pltpu.roll(value, shift, axis)


def field_part(refs, slots, field, rows, lanes):
    water, soak, terrain, land = refs
    if field < 2:
        return water[slots[field], 0, rows, lanes]
    if field < 4:
        return soak[slots[field - 2], 0, rows, lanes]
    if field == 4:
        return terrain[0, rows, lanes]
    return land[0, rows, lanes].astype(jnp.float32)


def columns_kernel(anc, *refs):
    first, last = refs[:4], refs[4:8]
    forcing, west_out, east_out, rain_out = refs[8:]
    slots = [anc[p] % 2 for p in range(2)]
    every = pl.ds(0, LANES)
    for h in range(HOURS):
        net = forcing[h, 0, 0].astype(jnp.float32) - forcing[h, 1, 0].astype(jnp.float32)
        rain_out[h] = coded(net, RAIN_SCALE).astype(jnp.int16)

    def edges(d, carry):
        rows = pl.ds(pl.multiple_of(d * SHARD, SHARD), SHARD)
        group = lane_ids(SHARD) // COLS
        to_west = jnp.zeros((SHARD, LANES), jnp.int32)
        to_east = jnp.zeros((SHARD, LANES), jnp.int32)
        for f in range(FIELDS):
            if f < ROW_FIELDS:
                a = coded(field_part(first, slots, f, rows, every), SCALES[f])
                b = coded(field_part(last, slots, f, rows, every), SCALES[f])
            else:
                a = rain_out[f - ROW_FIELDS, :, pl.ds(0, LANES)].astype(jnp.int32)
                b = rain_out[f - ROW_FIELDS, :, pl.ds(CX - LANES, LANES)].astype(jnp.int32)
            at = FROM_EAST[f]
            to_west = jnp.where(group == at, rolled(a, at * COLS), to_west)
            at = FROM_WEST[f]
            to_east = jnp.where(group == at, rolled(b, (at + 1) * COLS - LANES), to_east)
        west_out[rows, :] = to_west.astype(jnp.int16)
        east_out[rows, :] = to_east.astype(jnp.int16)
        return carry

    lax.fori_loop(0, CY // SHARD, edges, 0)


def rows_kernel(anc, *refs):
    first, last = refs[:4], refs[4:8]
    north_out, south_out, rows_n, rows_s = refs[8:]
    slots = [anc[p] % 2 for p in range(2)]
    rest = pl.ds(ROW_FIELDS * HALO, ROW_BLOCK - ROW_FIELDS * HALO)
    sixteen = pl.ds(0, 16)
    for c in range(CHUNKS):
        lanes = pl.ds(c * LANES, LANES)
        for f in range(ROW_FIELDS):
            put = pl.ds(HALO * f, HALO)
            rows_n[c, put, :] = coded(field_part(first, slots, f, sixteen, lanes), SCALES[f])[:HALO]
            rows_s[c, put, :] = coded(field_part(last, slots, f, sixteen, lanes), SCALES[f])[16 - HALO:]
        for ref, out in ((rows_n, north_out), (rows_s, south_out)):
            ref[c, rest, :] = jnp.zeros((ROW_BLOCK - ROW_FIELDS * HALO, LANES), jnp.int32)
            out[:, lanes] = ref[c].astype(jnp.int16)


def step_kernel(anc, owner, cond, suction, manning, prior, water_in, soak_in, terrain_in, land_in, rain_in, seen_in,
                east_in, west_in, north_in, south_in, rain_n, rain_s,
                depth_out, soak_out, misfit_out,
                water, soak, terrain, land, rain, seen, sems,
                nat, east, west, east_r, west_r, rows_ns, W, S, G, dgc, dgr, L, R, flux, coef):
    f32 = jnp.float32
    sources = (water_in, soak_in, terrain_in, land_in, rain_in, seen_in)
    copies = [
        pltpu.make_async_copy(src, dst, sems.at[i])
        for i, (src, dst) in enumerate(zip(sources, (water, soak, terrain, land, rain, seen)))
    ]
    for copy in copies:
        copy.start()
    slots = [anc[p] % 2 for p in range(2)]
    lane8 = lane_ids(8)
    lane_e = lane_ids(EXT)
    low = lane8 < 64
    last_lane = lane8 == LANES - 1
    first_lane = lane8 == 0
    body = pl.ds(HALO, CY)
    top = pl.ds(0, HALO)
    bottom = pl.ds(HALO + CY, HALO)
    every = pl.ds(0, EXT)

    corners = pl.ds(ROW_BLOCK, 16)
    for ref, of_rain, got, col in ((east, east_r, east_in, 0), (west, west_r, west_in, 1)):
        lanes = pl.ds(col * LANES, LANES)
        ref[body, :] = got[:, :].astype(jnp.int32)
        ref[top, :] = north_in[corners, lanes].astype(jnp.int32)[16 - HALO:]
        ref[bottom, :] = south_in[corners, lanes].astype(jnp.int32)[:HALO]
        early = pl.ds(col * 2 * LANES, LANES)
        late = pl.ds((col * 2 + 1) * LANES, LANES)
        of_rain[top, :] = rain_n[pl.ds(32, 16), late].astype(jnp.int32)[16 - HALO:]
        of_rain[bottom, :] = rain_s[pl.ds(32, 16), early].astype(jnp.int32)[:HALO]
    for c in range(CHUNKS):
        lanes = pl.ds(c * LANES, LANES)
        rows_ns[0, c] = north_in[pl.ds(0, ROW_BLOCK), lanes].astype(jnp.int32)
        rows_ns[1, c] = south_in[pl.ds(0, ROW_BLOCK), lanes].astype(jnp.int32)

    def decode(value, f):
        return value.astype(f32) * (1.0 / SCALES[f])

    def tile_rows(dest, f, fix=lambda v: v):
        for c in range(CHUNKS):
            lanes = pl.ds(c * LANES, LANES)
            if f < 2:
                dest[c, body, :] = water[slots[f], 0, :, lanes]
            elif f < 4:
                dest[c, body, :] = soak[slots[f - 2], 0, :, lanes]
            elif f == 4:
                dest[c, body, :] = terrain[0, :, lanes]
            elif f == 5:
                dest[c, body, :] = land[0, :, lanes].astype(f32)
            else:
                h = f - ROW_FIELDS
                for d in range(CY // SHARD):
                    dest[c, pl.ds(HALO + SHARD * d, SHARD), :] = decode(rain[d % 4, d // 4, pl.ds(SHARD * h, SHARD), lanes].astype(jnp.int32), f)
                dest[c, top, :] = decode(rain_n[pl.ds(16 * h, 16), lanes].astype(jnp.int32)[16 - HALO:], f)
                dest[c, bottom, :] = decode(rain_s[pl.ds(16 * h, 16), lanes].astype(jnp.int32)[:HALO], f)
                continue
            put = pl.ds(HALO * f, HALO)
            dest[c, top, :] = fix(decode(rows_ns[0, c, put, :], f))
            dest[c, bottom, :] = fix(decode(rows_ns[1, c, put, :], f))

    def column_halo(f0, f1, fill, fix=lambda v: v):
        group = lane_e // COLS
        x = jnp.full((EXT, LANES), fill, f32)
        e, w = (east, west) if f0 < ROW_FIELDS else (east_r, west_r)
        for f, ref, table, at in ((f1, e, FROM_EAST, 0), (f0, w, FROM_WEST, 3), (f0, e, FROM_EAST, 4), (f1, w, FROM_WEST, 7)):
            x = jnp.where(group == at, fix(decode(rolled(ref[...], (at - table[f]) * COLS), f)), x)
        nat[CHUNKS] = x

    def tiles(step, per=5):
        def some(i, carry):
            for u in range(per):
                step(pl.multiple_of((i * per + u) * 8, 8))
            return carry

        lax.fori_loop(0, EXT // (8 * per), some, 0)

    def ring(dest, copy, fix=lambda v, c, rows: v):
        def one(at):
            rows = pl.ds(at, 8)
            v = [nat[c, rows, :] for c in range(CHUNKS + 1)]
            if copy:
                for c in range(CHUNKS):
                    dest[c, rows, :] = fix(v[c], c, rows)
            v = [rolled(t, 64) for t in v]
            for k in range(CHUNKS + 1):
                dest[CHUNKS + k, rows, :] = fix(jnp.where(low, v[k - 1], v[k]), CHUNKS + k, rows)

        tiles(one)

    column_halo(0, 1, 0.0)
    copies[0].wait()
    tile_rows(W, 0)
    tile_rows(nat, 1)
    ring(W, False)
    guard = lambda v: jnp.maximum(v, 0.1)
    column_halo(2, 3, 1.0, guard)
    copies[1].wait()
    tile_rows(S, 2, guard)
    tile_rows(nat, 3, guard)
    ring(S, False)
    column_halo(4, 4, 0.0)
    copies[2].wait()
    tile_rows(nat, 4)
    ring(G, True)
    column_halo(5, 5, 0.0)
    copies[3].wait()
    tile_rows(nat, 5)
    ring(L, True)
    copies[4].wait()
    for of_rain, col in ((east_r, 0), (west_r, 1)):
        for d in range(CY // SHARD):
            for half in range(2):
                lanes = pl.ds((col * 2 + half) * LANES, LANES)
                part = rain[d % 4, d // 4, pl.ds(2 * SHARD, 16), lanes]
                of_rain[pl.ds(HALO + SHARD * d + 16 * half, 16), :] = part.astype(jnp.int32)
    for h in range(HOURS):
        column_halo(6 + h, 6 + h, 0.0)
        tile_rows(nat, 6 + h)
        ring(R.at[h], True, lambda v, c, rows: jnp.where(L[c, rows, :] > 0.0, v * TIME_STEP, WATER_BODY))
    for c in range(WIDE):
        for ref in (W, G):
            ref[c, pl.ds(EXT, 8), :] = jnp.zeros((8, LANES), f32)
        flux[c, pl.ds(0, 8), :] = jnp.zeros((8, LANES), f32)

    def ground_steps(at):
        rows = pl.ds(at, 8)
        g = [G[c, rows, :] for c in range(WIDE)]
        r = [rolled(v, -1) for v in g]
        for c in range(WIDE):
            dgc[c, rows, :] = jnp.where(last_lane, r[(c + 1) % WIDE], r[c]) - g[c]
            dgr[c, rows, :] = G[c, pl.ds(at + 1, 8), :] - g[c]

    tiles(ground_steps)

    for k in range(3):
        pair = []
        for p in range(2):
            o = owner[slots[p]]
            if k == 0:
                pair.append(jnp.full((8, LANES), TIME_STEP * 0.5 ** (5.0 / 3.0), f32) / jnp.full((8, LANES), manning[o], f32))
            elif k == 1:
                pair.append(jnp.full((8, LANES), TIME_STEP * cond[o], f32))
            else:
                pair.append(jnp.full((8, LANES), TIME_STEP * cond[o] * suction[o], f32))
        for c in range(WIDE):
            v = pair[0] if c < CHUNKS else pair[1]
            if c == CHUNKS:
                v = jnp.where(lane8 < 32, pair[0], pair[1])
            if c == WIDE - 1:
                v = jnp.where(lane8 < 96, pair[1], pair[0])
            coef[k, c] = v

    def face(a, b, dg):
        total = a + b
        slope = (b - a) + dg
        return jnp.exp2(lax.log2(total) * (5.0 / 3.0)) * slope * lax.rsqrt(jnp.abs(slope) + SLOPE_FLOOR)

    def substep(h):
        def one(at):
            rows = pl.ds(at, 8)
            w = [W[c, rows, :] for c in range(WIDE)]
            r = [rolled(v, -1) for v in w]
            fe = [face(w[c], jnp.where(last_lane, r[(c + 1) % WIDE], r[c]), dgc[c, rows, :]) for c in range(WIDE)]
            r = [rolled(v, 1) for v in fe]
            for c in range(WIDE):
                fw = jnp.where(first_lane, r[c - 1], r[c])
                fs = face(w[c], W[c, pl.ds(at + 1, 8), :], dgr[c, rows, :])
                flux[c, pl.ds(at + 8, 8), :] = fs
                gain = (fe[c] - fw) + (fs - flux[c, pl.ds(at + 7, 8), :])
                ponded = jnp.maximum(w[c] + coef[0, c] * gain + R[h, c, rows, :], 0.0)
                s = S[c, rows, :]
                intake = jnp.minimum(coef[1, c] + coef[2, c] / s, ponded)
                W[c, rows, :] = ponded - intake
                S[c, rows, :] = s + intake

        tiles(one, TILES)

    def slot_one(ref, rows):
        v = [rolled(ref[CHUNKS + k, rows, :], 64) for k in range(CHUNKS + 1)]
        return [jnp.where(low, v[k], v[k + 1]) for k in range(CHUNKS)]

    def hour(h, total):
        lax.fori_loop(0, SUB, lambda i, carry: (substep(h), carry)[1], 0)

        def score(i, total):
            total = list(total)
            for half in range(2):
                start = pl.multiple_of(i * 16, 16)
                rows = pl.ds(start + half * 8, 8)
                inner = pl.ds(start + half * 8 + HALO, 8)
                ones = slot_one(W, inner)
                for c in range(CHUNKS):
                    lanes = pl.ds(c * LANES, LANES)
                    o = seen[h, 0, pl.ds(start, 16), lanes].astype(f32)[half * 8:half * 8 + 8]
                    keep = land[0, rows, lanes].astype(f32)
                    total[2] = total[2] + keep
                    for p, v in enumerate((W[c, inner, :], ones[c])):
                        depth_out[p, 0, rows, lanes] = v
                        gap = v - o
                        square = gap * gap
                        total[p] = total[p] + keep * square / (1.0 + square)
            return tuple(total)

        return lax.fori_loop(0, CY // 16, score, total)

    copies[5].wait()
    zero = jnp.zeros((8, LANES), f32)
    one, two, cells = lax.fori_loop(0, HOURS, hour, (zero, zero, zero))

    def wet(i, carry):
        for u in range(4):
            start = pl.multiple_of((i * 4 + u) * 8, 8)
            rows = pl.ds(start, 8)
            inner = pl.ds(start + HALO, 8)
            ones = slot_one(S, inner)
            for c in range(CHUNKS):
                lanes = pl.ds(c * LANES, LANES)
                soak_out[0, 0, rows, lanes] = S[c, inner, :]
                soak_out[1, 0, rows, lanes] = ones[c]
        return carry

    lax.fori_loop(0, CY // 32, wet, 0)
    line = lane_ids(1)
    misfit_out[...] = jnp.where(
        line == 0,
        jnp.sum(one),
        jnp.where(line == 1, jnp.sum(two), jnp.where(line == 2, jnp.sum(cells), (prior[0] + prior[1]) * 0.5)),
    )


VM = pl.BlockSpec(memory_space=pltpu.VMEM)
SM = pl.BlockSpec(memory_space=pltpu.SMEM)


def ends(shape, where):
    pair = pl.BlockSpec((2, 1) + shape, lambda i: (0, 0) + where)
    one = pl.BlockSpec((1,) + shape, lambda i: (0,) + where)
    return [pair, pair, one, one]


def whole(shape):
    return pl.BlockSpec(shape, lambda i: (0,) * len(shape))


def pack_columns(anc, fields, forcing):
    shapes = [(CY, LANES), (CY, LANES), (HOURS, SHARD, CX)]
    return pl.pallas_call(
        columns_kernel,
        out_shape=[jax.ShapeDtypeStruct(shape, jnp.int16) for shape in shapes],
        grid=(1,),
        in_specs=[SM] + ends((CY, LANES), (0, 0)) + ends((CY, LANES), (0, CHUNKS - 1)) + [whole(forcing.shape)],
        out_specs=[whole(shape) for shape in shapes],
        name="pack_columns",
    )(anc, *fields, *fields, forcing)


def pack_rows(anc, fields):
    shape = (ROW_BLOCK, CX)
    return pl.pallas_call(
        rows_kernel,
        out_shape=[jax.ShapeDtypeStruct(shape, jnp.int16)] * 2,
        grid=(1,),
        in_specs=[SM] + ends((16, CX), (0, 0)) + ends((16, CX), (CY // 16 - 1, 0)),
        out_specs=[whole(shape)] * 2,
        scratch_shapes=[pltpu.VMEM((CHUNKS, ROW_BLOCK, LANES), jnp.int32)] * 2,
        name="pack_rows",
    )(anc, *fields, *fields)


def steps(*args):
    f32 = jnp.float32
    wide = pltpu.VMEM((WIDE, EXT, LANES), f32)
    tall = pltpu.VMEM((WIDE, EXT + 8, LANES), f32)
    return pl.pallas_call(
        step_kernel,
        out_shape=(
            jax.ShapeDtypeStruct((2, 1, CY, CX), f32),
            jax.ShapeDtypeStruct((2, 1, CY, CX), f32),
            jax.ShapeDtypeStruct((1, LANES), f32),
        ),
        in_specs=[SM] * 6 + [pl.BlockSpec(memory_space=pltpu.HBM)] * 6 + [VM] * 6,
        out_specs=(VM,) * 3,
        scratch_shapes=[pltpu.VMEM(x.shape, x.dtype) for x in args[6:12]]
        + [
            pltpu.SemaphoreType.DMA((6,)),
            pltpu.VMEM((CHUNKS + 1, EXT, LANES), f32),
            pltpu.VMEM((EXT, LANES), jnp.int32),
            pltpu.VMEM((EXT, LANES), jnp.int32),
            pltpu.VMEM((EXT, LANES), jnp.int32),
            pltpu.VMEM((EXT, LANES), jnp.int32),
            pltpu.VMEM((2, CHUNKS, ROW_BLOCK, LANES), jnp.int32),
            tall, wide, tall, wide, wide, wide,
            pltpu.VMEM((HOURS, WIDE, EXT, LANES), f32),
            tall,
            pltpu.VMEM((3, WIDE, 8, LANES), f32),
        ],
        compiler_params=pltpu.CompilerParams(vmem_limit_bytes=40 << 20),
        name="steps",
    )(*args)


def route(down, right):
    pairs = []
    rows = lax.axis_size("space") // TX
    for r in range(rows):
        for c in range(TX):
            if 0 <= r + down < rows:
                pairs.append((r * TX + c, (r + down) * TX + (c + right) % TX))
    return pairs


def window(water, soak, terrain, land, forcing, seen, cond, suction, manning, owner, anc, prior):
    groups = lax.axis_size("dom")
    tiles = lax.axis_size("space")
    fields = (water, soak, terrain, land)
    to_west, to_east, rain = pack_columns(anc, fields, forcing)
    from_east = lax.ppermute(to_west, "space", route(0, -1))
    from_west = lax.ppermute(to_east, "space", route(0, 1))
    to_north, to_south = pack_rows(anc, fields)

    shard = jnp.concatenate([from_east[:16], from_east[16:32], from_west[:16], from_west[16:32]], axis=1)
    shard = jnp.concatenate([rain.reshape(HOURS * SHARD, CX), shard], axis=0)
    line = groups // 2
    partner = lax.ppermute(shard, "dom", [(i, (i + line) % groups) for i in range(groups)])

    def with_corners(block, rows):
        corner = jnp.concatenate([from_east[rows], from_west[rows]] * 2, axis=1)
        return jnp.concatenate([block, corner], axis=0)

    from_south = lax.ppermute(with_corners(to_north, slice(0, 16)), "space", route(-1, 0))
    from_north = lax.ppermute(with_corners(to_south, slice(CY - 16, CY)), "space", route(1, 0))
    upper = lax.axis_index("dom") >= line
    pair = jnp.stack([jnp.where(upper, partner, shard), jnp.where(upper, shard, partner)])
    lines = [list(range(line)), list(range(line, groups))]
    rain = lax.all_to_all(jnp.broadcast_to(pair[None], (line,) + pair.shape), "dom", 0, 0, axis_index_groups=lines, tiled=True)

    a, b = rain[0, 0], rain[-1, -1]
    rain_south = lax.ppermute(jnp.concatenate([a[0:16], a[32:48], a[64:80]], axis=0), "space", route(-1, 0))
    rain_north = lax.ppermute(jnp.concatenate([b[16:32], b[48:64], b[64:80]], axis=0), "space", route(1, 0))

    depth, wet, score = steps(anc, owner, cond, suction, manning, prior, water, soak, terrain, land, rain, seen,
                              from_east, from_west, from_north, from_south, rain_north, rain_south)

    score = score + lax.ppermute(score, "space", [(i, i ^ 1) for i in range(tiles)])
    peers = [[t * groups + d for t in range(k, tiles, 2) for d in range(groups)] for k in range(2)]
    line = jnp.broadcast_to(score[None], (tiles // 2 * groups, 1, LANES))
    line = lax.all_to_all(line, ("space", "dom"), 0, 0, axis_index_groups=peers, tiled=True)
    line = line.reshape(tiles // 2, groups, LANES)
    table = jnp.sum(line, axis=0)
    raw = 0.5 * line[0, :, 3:4] * jnp.exp(-SHARPNESS * table[:, :2] / table[:, 2:3])
    weights = raw / jnp.sum(raw)
    mine = lax.broadcasted_iota(jnp.int32, (groups, 1), 0) == lax.axis_index("dom")
    return depth, wet, jnp.sum(jnp.where(mine, weights, 0.0), axis=0)


def solution(mesh):
    return jax.shard_map(
        window,
        mesh=mesh,
        in_specs=(
            P("dom", "space", None, None),
            P("dom", "space", None, None),
            P("space", None, None),
            P("space", None, None),
            P(None, None, "space", "dom", None),
            P(None, "space", None, None),
            P(),
            P(),
            P(),
            P("dom"),
            P("dom"),
            P("dom"),
        ),
        out_specs=(P("dom", "space", None, None), P("dom", "space", None, None), P("dom")),
        check_vma=False,
    )
```

profile of v0, /device:TPU:1, one launch (start us, length us, event | category | flops | bytes accessed | tf_op | source)
XLA Modules:
  0.0 123.1 jit_solution(6980517607960222135)
XLA Ops:
  0.6 3.2 %pack_columns.1 = (s16[256,128]{1,0:T(8,128)(2,1)}, s16[256,128]{1,0:T(8,128)(2,1)}, s16[2,32,512]{2,1,0:T(8,128)(2,1)}) custom-call(s32[2]{0:T(128)} %anc.5, f32[2,1,256,512]{3,2,1,0:T(8,128)} %water_in.1, f32[2,1,256,512]{3,2,1,0:T(8,128)} %soak_in.1, f32[1,256,512]{2,1,0:T(8,128)} %terrain_in.1, s32[1,256,512]{2,1,0:T(8,128)} %land_in.1, ...), custom_call_target="tpu_custom_call" | custom-call | tf_op jit(solution)/shard_map/pack_columns/pallas_call | solution.py:364
  3.9 3.2 %collective-permute-start = (s16[256,128]{1,0:T(8,128)(2,1)}, s16[256,128]{1,0:T(8,128)(2,1)S(1)}, u32[]{:S(2)}, u32[]{:S(2)}) collective-permute-start(s16[256,128]{1,0:T(8,128)(2,1)} %get-tuple-element.12), channel_id=1, source_target_pairs={{0,24},{8,0},{16,8},{24,16},{32,56},{40,32},{48,40},{56,48},{64,88... | collective-permute-start | bytes 196616 | tf_op jit(solution)/shard_map/ppermute | solution.py:434
  7.1 0.0 collective-permute-start.1
  7.1 1.6 %collective-permute-done.east_in = s16[256,128]{1,0:T(8,128)(2,1)S(1)} collective-permute-done((s16[256,128]{1,0:T(8,128)(2,1)}, s16[256,128]{1,0:T(8,128)(2,1)S(1)}, u32[]{:S(2)}, u32[]{:S(2)}) %collective-permute-start) | collective-permute-done | bytes 65568 | tf_op jit(solution)/shard_map/ppermute | solution.py:434
  8.7 0.4 collective-permute-done.1.west_in
  9.1 0.9 add_add_fusion.2
  10.0 6.6 %collective-permute-start.2 = (s16[80,512]{1,0:T(8,128)(2,1)S(1)}, s16[80,512]{1,0:T(8,128)(2,1)S(1)}, u32[]{:S(2)}, u32[]{:S(2)}) collective-permute-start(s16[80,512]{1,0:T(8,128)(2,1)S(1)} %add_add_fusion.2), channel_id=1, source_target_pairs={{0,4},{1,5},{2,6},{3,7},{4,0},{5,1},{6,2},{7,3},{8,12},{9,13},{10,... | collective-permute-start | bytes 245768 | tf_op jit(solution)/shard_map/ppermute | solution.py:441
  16.6 1.9 %collective-permute-done.2 = s16[80,512]{1,0:T(8,128)(2,1)S(1)} collective-permute-done((s16[80,512]{1,0:T(8,128)(2,1)S(1)}, s16[80,512]{1,0:T(8,128)(2,1)S(1)}, u32[]{:S(2)}, u32[]{:S(2)}) %collective-permute-start.2) | collective-permute-done | bytes 81952 | tf_op jit(solution)/shard_map/ppermute | solution.py:441
  18.6 0.9 broadcast_in_dim.26
  19.5 4.2 %all-to-all-start = ((s16[4,2,80,512]{3,2,1,0:T(8,128)(2,1)}), s16[4,2,80,512]{3,2,1,0:T(8,128)(2,1)}, u32[]{:S(2)}, u32[]{:S(2)}) async-start(s16[4,2,80,512]{3,2,1,0:T(8,128)(2,1)} %broadcast_in_dim.26), calls=%async_computation | async-start | bytes 1310720 | tf_op jit(solution)/shard_map/all_to_all | solution.py:452
  23.7 0.0 copy-start
  23.7 0.0 copy-start.1
  23.7 0.0 copy-start.3
  23.7 1.9 %pack_rows.1 = (s16[80,512]{1,0:T(8,128)(2,1)}, s16[80,512]{1,0:T(8,128)(2,1)}) custom-call(s32[2]{0:T(128)} %anc.5, f32[2,1,256,512]{3,2,1,0:T(8,128)} %water_in.1, f32[2,1,256,512]{3,2,1,0:T(8,128)} %soak_in.1, f32[1,256,512]{2,1,0:T(8,128)} %terrain_in.1, s32[1,256,512]{2,1,0:T(8,128)} %land_in.1, f32[2,1,256,512]{3,2,1,0:T(8,128)} %water_in.1, ...), custom_call_target="tpu_custom_call" | custom-call | tf_op jit(solution)/shard_map/pack_rows/pallas_call | solution.py:376
  25.7 1.6 %add_add_fusion.1 = s16[96,512]{1,0:T(8,128)(2,1)} fusion(s16[16,128]{1,0:T(8,128)(2,1)S(1)} %get-tuple-element.34, s16[16,128]{1,0:T(8,128)(2,1)S(1)} %get-tuple-element.31, s16[80,512]{1,0:T(8,128)(2,1)} %get-tuple-element.15), kind=kLoop, calls=%fused_computation.2 | loop fusion | flops 196608 | bytes 188416 | tf_op jit(solution)/shard_map/concatenate | solution.py:445
  27.3 1.3 %collective-permute-start.4 = (s16[96,512]{1,0:T(8,128)(2,1)}, s16[96,512]{1,0:T(8,128)(2,1)S(1)}, u32[]{:S(2)}, u32[]{:S(2)}) collective-permute-start(s16[96,512]{1,0:T(8,128)(2,1)} %add_add_fusion.1), channel_id=1, source_target_pairs={{32,0},{40,8},{48,16},{56,24},{64,32},{72,40},{80,48},{88,56},{96,... | collective-permute-start | bytes 294920 | tf_op jit(solution)/shard_map/ppermute | solution.py:447
  28.6 1.5 %add_add_fusion = s16[96,512]{1,0:T(8,128)(2,1)} fusion(s16[16,128]{1,0:T(8,128)(2,1)S(1)} %get-tuple-element.32, s16[16,128]{1,0:T(8,128)(2,1)S(1)} %get-tuple-element.29, s16[80,512]{1,0:T(8,128)(2,1)} %get-tuple-element.14), kind=kLoop, calls=%fused_computation.1 | loop fusion | flops 196608 | bytes 188416 | tf_op jit(solution)/shard_map/concatenate | solution.py:445
  30.1 5.5 %collective-permute-start.3 = (s16[96,512]{1,0:T(8,128)(2,1)}, s16[96,512]{1,0:T(8,128)(2,1)S(1)}, u32[]{:S(2)}, u32[]{:S(2)}) collective-permute-start(s16[96,512]{1,0:T(8,128)(2,1)} %add_add_fusion), channel_id=1, source_target_pairs={{0,32},{8,40},{16,48},{24,56},{32,64},{40,72},{48,80},{56,88},{64,... | collective-permute-start | bytes 294920 | tf_op jit(solution)/shard_map/ppermute | solution.py:448
  35.6 0.0 all-to-all-done.rain_in
  35.6 0.8 slice_bitcast_fusion.2
  36.4 5.5 %collective-permute-start.5 = (s16[48,512]{1,0:T(8,128)(2,1)S(1)}, s16[48,512]{1,0:T(8,128)(2,1)S(1)}, u32[]{:S(2)}, u32[]{:S(2)}) collective-permute-start(s16[48,512]{1,0:T(8,128)(2,1)S(1)} %pad_add_fusion.1), channel_id=1, source_target_pairs={{0,32},{8,40},{16,48},{24,56},{32,64},{40,72},{48,80},{56,88},{64,... | collective-permute-start | bytes 147464 | tf_op jit(solution)/shard_map/ppermute | solution.py:456
  41.9 0.0 copy-start.5
  41.9 0.0 copy-start.6
  42.0 0.0 copy-start.7
  42.0 0.0 copy-start.8
  42.0 0.0 copy-start.9
  42.0 0.0 copy-start.10
  42.0 1.3 %collective-permute-start.6 = (s16[48,512]{1,0:T(8,128)(2,1)S(1)}, s16[48,512]{1,0:T(8,128)(2,1)S(1)}, u32[]{:S(2)}, u32[]{:S(2)}) collective-permute-start(s16[48,512]{1,0:T(8,128)(2,1)S(1)} %pad_add_fusion.2), channel_id=1, source_target_pairs={{32,0},{40,8},{48,16},{56,24},{64,32},{72,40},{80,48},{88,56},{96,... | collective-permute-start | bytes 147464 | tf_op jit(solution)/shard_map/ppermute | solution.py:455
  43.3 0.0 collective-permute-done.4.south_in
  43.3 0.0 collective-permute-done.3.north_in
  43.3 0.0 collective-permute-done.5.rain_n
  43.3 5.0 %collective-permute-done.6.rain_s = s16[48,512]{1,0:T(8,128)(2,1)S(1)} collective-permute-done((s16[48,512]{1,0:T(8,128)(2,1)S(1)}, s16[48,512]{1,0:T(8,128)(2,1)S(1)}, u32[]{:S(2)}, u32[]{:S(2)}) %collective-permute-start.6) | collective-permute-done | bytes 49184 | tf_op jit(solution)/shard_map/ppermute | solution.py:455
  48.4 0.0 copy-done.2
  48.4 0.0 copy-done.5
  48.4 0.0 copy-done.6
  48.4 0.0 copy-done.7
  48.4 0.0 copy-start.4
  48.4 1.0 copy-done.4
  49.5 40.7 %steps.1 = (f32[2,1,256,512]{3,2,1,0:T(8,128)}, f32[2,1,256,512]{3,2,1,0:T(8,128)}, f32[1,128]{1,0:T(1,128)S(1)}) custom-call(s32[2]{0:T(128)S(1)} %copy-done.5, s32[2]{0:T(128)S(1)} %copy-done.6, f32[16]{0:T(128)S(1)} %copy-done.7, f32[16]{0:T(128)S(1)} %copy-done.8, f32[16]{0:T(128)S(1)} %copy-done.9, f32[2]{0:T(128)S(1)} %copy-done.10, ...), custom_call_target="tpu_custom_call" | custom-call | tf_op jit(solution)/shard_map/steps/pallas_call | solution.py:391
  90.2 4.4 %collective-permute-start.7 = (f32[1,128]{1,0:T(1,128)S(1)}, f32[1,128]{1,0:T(1,128)S(1)}, u32[]{:S(2)}, u32[]{:S(2)}) collective-permute-start(f32[1,128]{1,0:T(1,128)S(1)} %get-tuple-element.18), channel_id=1, source_target_pairs={{0,8},{8,0},{16,24},{24,16},{32,40},{40,32},{48,56},{56,48},{64,72... | collective-permute-start | bytes 1544 | tf_op jit(solution)/shard_map/ppermute | solution.py:461
  94.6 0.8 collective-permute-done.7
  95.4 0.7 broadcast_in_dim.29
  96.1 14.7 %all-to-all-start.1 = ((f32[128,1,128]{2,1,0:T(1,128)}), f32[128,1,128]{2,1,0:T(1,128)S(1)}, u32[]{:S(2)}, u32[]{:S(2)}) async-start(f32[128,1,128]{2,1,0:T(1,128)} %broadcast_in_dim.29), calls=%async_computation.1 | async-start | bytes 131072 | tf_op jit(solution)/shard_map/all_to_all | solution.py:464
  110.8 10.1 %all-to-all-done.1 = f32[128,1,128]{2,1,0:T(1,128)S(1)} async-done(((f32[128,1,128]{2,1,0:T(1,128)}), f32[128,1,128]{2,1,0:T(1,128)S(1)}, u32[]{:S(2)}, u32[]{:S(2)}) %all-to-all-start.1) | async-done | bytes 65568 | tf_op jit(solution)/shard_map/all_to_all | solution.py:464
  120.9 0.2 fusion
  121.1 0.2 slice_reduce_fusion
  121.3 0.7 fusion.1
  122.0 1.1 select_reduce_fusion
  (18 shorter events, 0.1 us)
Async XLA Ops:
  3.9 4.8 %collective-permute-start = (s16[256,128]{1,0:T(8,128)(2,1)}, s16[256,128]{1,0:T(8,128)(2,1)S(1)}, u32[]{:S(2)}, u32[]{:S(2)}) collective-permute-start(s16[256,128]{1,0:T(8,128)(2,1)} %get-tuple-element.12), channel_id=1, source_target_pairs={{0,24},{8,0},{16,8},{24,16},{32,56},{40,32},{48,40},{56,48},{64,88... | collective-permute-start | bytes 196616 | tf_op jit(solution)/shard_map/ppermute | solution.py:434
  7.1 2.1 %collective-permute-start.1 = (s16[256,128]{1,0:T(8,128)(2,1)}, s16[256,128]{1,0:T(8,128)(2,1)S(1)}, u32[]{:S(2)}, u32[]{:S(2)}) collective-permute-start(s16[256,128]{1,0:T(8,128)(2,1)} %get-tuple-element.13), channel_id=1, source_target_pairs={{0,8},{8,16},{16,24},{24,0},{32,40},{40,48},{48,56},{56,32},{64,72... | collective-permute-start | bytes 196616 | tf_op jit(solution)/shard_map/ppermute | solution.py:435
  9.1 9.5 %copy-start.11 = (s16[2,32,512]{2,1,0:T(8,128)(2,1)S(1)}, s16[2,32,512]{2,1,0:T(8,128)(2,1)}, u32[]{:S(2)}) copy-start(s16[2,32,512]{2,1,0:T(8,128)(2,1)} %get-tuple-element.11) | copy-start | bytes 196612
  10.0 8.5 %collective-permute-start.2 = (s16[80,512]{1,0:T(8,128)(2,1)S(1)}, s16[80,512]{1,0:T(8,128)(2,1)S(1)}, u32[]{:S(2)}, u32[]{:S(2)}) collective-permute-start(s16[80,512]{1,0:T(8,128)(2,1)S(1)} %add_add_fusion.2), channel_id=1, source_target_pairs={{0,4},{1,5},{2,6},{3,7},{4,0},{5,1},{6,2},{7,3},{8,12},{9,13},{10,... | collective-permute-start | bytes 245768 | tf_op jit(solution)/shard_map/ppermute | solution.py:441
  19.5 16.1 %all-to-all-start = ((s16[4,2,80,512]{3,2,1,0:T(8,128)(2,1)}), s16[4,2,80,512]{3,2,1,0:T(8,128)(2,1)}, u32[]{:S(2)}, u32[]{:S(2)}) async-start(s16[4,2,80,512]{3,2,1,0:T(8,128)(2,1)} %broadcast_in_dim.26), calls=%async_computation | async-start | bytes 1310720 | tf_op jit(solution)/shard_map/all_to_all | solution.py:452
  23.7 24.6 %copy-start = (f32[2,1,256,512]{3,2,1,0:T(8,128)S(1)}, f32[2,1,256,512]{3,2,1,0:T(8,128)}, u32[]{:S(2)}) copy-start(f32[2,1,256,512]{3,2,1,0:T(8,128)} %water_in.1) | copy-start | bytes 3145732
  23.7 24.6 %copy-start.1 = (f32[2,1,256,512]{3,2,1,0:T(8,128)S(1)}, f32[2,1,256,512]{3,2,1,0:T(8,128)}, u32[]{:S(2)}) copy-start(f32[2,1,256,512]{3,2,1,0:T(8,128)} %soak_in.1) | copy-start | bytes 3145732
  23.7 24.6 %copy-start.3 = (s32[1,256,512]{2,1,0:T(8,128)S(1)}, s32[1,256,512]{2,1,0:T(8,128)}, u32[]{:S(2)}) copy-start(s32[1,256,512]{2,1,0:T(8,128)} %land_in.1) | copy-start | bytes 1572868
  25.7 22.7 %copy-start.2 = (f32[1,256,512]{2,1,0:T(8,128)S(1)}, f32[1,256,512]{2,1,0:T(8,128)}, u32[]{:S(2)}) copy-start(f32[1,256,512]{2,1,0:T(8,128)} %terrain_in.1) | copy-start | bytes 1572868
  27.3 16.0 %collective-permute-start.4 = (s16[96,512]{1,0:T(8,128)(2,1)}, s16[96,512]{1,0:T(8,128)(2,1)S(1)}, u32[]{:S(2)}, u32[]{:S(2)}) collective-permute-start(s16[96,512]{1,0:T(8,128)(2,1)} %add_add_fusion.1), channel_id=1, source_target_pairs={{32,0},{40,8},{48,16},{56,24},{64,32},{72,40},{80,48},{88,56},{96,... | collective-permute-start | bytes 294920 | tf_op jit(solution)/shard_map/ppermute | solution.py:447
  30.1 13.2 %collective-permute-start.3 = (s16[96,512]{1,0:T(8,128)(2,1)}, s16[96,512]{1,0:T(8,128)(2,1)S(1)}, u32[]{:S(2)}, u32[]{:S(2)}) collective-permute-start(s16[96,512]{1,0:T(8,128)(2,1)} %add_add_fusion), channel_id=1, source_target_pairs={{0,32},{8,40},{16,48},{24,56},{32,64},{40,72},{48,80},{56,88},{64,... | collective-permute-start | bytes 294920 | tf_op jit(solution)/shard_map/ppermute | solution.py:448
  36.4 6.9 %collective-permute-start.5 = (s16[48,512]{1,0:T(8,128)(2,1)S(1)}, s16[48,512]{1,0:T(8,128)(2,1)S(1)}, u32[]{:S(2)}, u32[]{:S(2)}) collective-permute-start(s16[48,512]{1,0:T(8,128)(2,1)S(1)} %pad_add_fusion.1), channel_id=1, source_target_pairs={{0,32},{8,40},{16,48},{24,56},{32,64},{40,72},{48,80},{56,88},{64,... | collective-permute-start | bytes 147464 | tf_op jit(solution)/shard_map/ppermute | solution.py:456
  41.9 6.4 %copy-start.5 = (s32[2]{0:T(128)S(1)}, s32[2]{0:T(128)}, u32[]{:S(2)}) copy-start(s32[2]{0:T(128)} %anc.5) | copy-start | bytes 28
  41.9 6.4 %copy-start.6 = (s32[2]{0:T(128)S(1)}, s32[2]{0:T(128)}, u32[]{:S(2)}) copy-start(s32[2]{0:T(128)} %owner.1) | copy-start | bytes 28
  42.0 6.4 %copy-start.7 = (f32[16]{0:T(128)S(1)}, f32[16]{0:T(128)}, u32[]{:S(2)}) copy-start(f32[16]{0:T(128)} %cond.1) | copy-start | bytes 196
  42.0 6.4 %copy-start.8 = (f32[16]{0:T(128)S(1)}, f32[16]{0:T(128)}, u32[]{:S(2)}) copy-start(f32[16]{0:T(128)} %suction.1) | copy-start | bytes 196
  42.0 6.4 %copy-start.9 = (f32[16]{0:T(128)S(1)}, f32[16]{0:T(128)}, u32[]{:S(2)}) copy-start(f32[16]{0:T(128)} %manning.1) | copy-start | bytes 196
  42.0 6.4 %copy-start.10 = (f32[2]{0:T(128)S(1)}, f32[2]{0:T(128)}, u32[]{:S(2)}) copy-start(f32[2]{0:T(128)} %prior.1) | copy-start | bytes 28
  42.0 6.3 %collective-permute-start.6 = (s16[48,512]{1,0:T(8,128)(2,1)S(1)}, s16[48,512]{1,0:T(8,128)(2,1)S(1)}, u32[]{:S(2)}, u32[]{:S(2)}) collective-permute-start(s16[48,512]{1,0:T(8,128)(2,1)S(1)} %pad_add_fusion.2), channel_id=1, source_target_pairs={{32,0},{40,8},{48,16},{56,24},{64,32},{72,40},{80,48},{88,56},{96,... | collective-permute-start | bytes 147464 | tf_op jit(solution)/shard_map/ppermute | solution.py:455
  48.4 1.0 copy-start.4
  90.2 5.2 %collective-permute-start.7 = (f32[1,128]{1,0:T(1,128)S(1)}, f32[1,128]{1,0:T(1,128)S(1)}, u32[]{:S(2)}, u32[]{:S(2)}) collective-permute-start(f32[1,128]{1,0:T(1,128)S(1)} %get-tuple-element.18), channel_id=1, source_target_pairs={{0,8},{8,0},{16,24},{24,16},{32,40},{40,32},{48,56},{56,48},{64,72... | collective-permute-start | bytes 1544 | tf_op jit(solution)/shard_map/ppermute | solution.py:461
  96.1 24.8 %all-to-all-start.1 = ((f32[128,1,128]{2,1,0:T(1,128)}), f32[128,1,128]{2,1,0:T(1,128)S(1)}, u32[]{:S(2)}, u32[]{:S(2)}) async-start(f32[128,1,128]{2,1,0:T(1,128)} %broadcast_in_dim.29), calls=%async_computation.1 | async-start | bytes 131072 | tf_op jit(solution)/shard_map/all_to_all | solution.py:464
where the time goes:
time: 124 us; the launch traced here: 123 us
  starting transfers between devices  46.7 us (38%)
  Pallas kernels  45.8 us (37%)
  waiting for transfers between devices  19.9 us (16%)
  other arithmetic  6.12 us (5%)
  local copies, waits for them, and re-layouts  3.66 us (3%)
    pallas_call x1, Pallas kernels, steps(): pl.pallas_call(step_kernel, out_shape=(jax.ShapeDtypeStruct((2, 1, CY, CX...  40.7 us
    all_to_all x1, starting transfers between devices, window(): lax.all_to_all(line, ('space', 'dom'), 0, 0, axis_index_groups=peers, til...  14.7 us
    all_to_all x1, waiting for transfers between devices, window(): lax.all_to_all(line, ('space', 'dom'), 0, 0, axis_index_groups=peers, til...  10.1 us
    ppermute x1, starting transfers between devices, window(): lax.ppermute(shard, 'dom', [(i, (i + line) % groups) for i in range(group...  6.61 us
    ppermute x1, starting transfers between devices, window(): lax.ppermute(jnp.concatenate([b[16:32], b[48:64], b[64:80]], axis=0), 'sp...  5.49 us
    ppermute x1, starting transfers between devices, window(): lax.ppermute(with_corners(to_south, slice(CY - 16, CY)), 'space', route(1...  5.48 us
    ppermute x1, waiting for transfers between devices, window(): lax.ppermute(jnp.concatenate([a[0:16], a[32:48], a[64:80]], axis=0), 'spa...  5.01 us
    ppermute x1, starting transfers between devices, window(): lax.ppermute(score, 'space', [(i, i ^ 1) for i in range(tiles)])  4.42 us
  transfers between devices with their start and end apart: 10, of which 6 were waited for; matrix products, arithmetic and copies ran while one was open for 3% of the time, Pallas kernels for 2%

commit v1 on v0

--- a/solution.py
+++ b/solution.py
@@ -108,136 +108,97 @@
             rows_s[c, put, :] = coded(field_part(last, slots, f, sixteen, lanes), SCALES[f])[16 - HALO:]
         for ref, out in ((rows_n, north_out), (rows_s, south_out)):
             ref[c, rest, :] = jnp.zeros((ROW_BLOCK - ROW_FIELDS * HALO, LANES), jnp.int32)
-            out[:, lanes] = ref[c].astype(jnp.int16)
-
-
-def step_kernel(anc, owner, cond, suction, manning, prior, water_in, soak_in, terrain_in, land_in, rain_in, seen_in,
-                east_in, west_in, north_in, south_in, rain_n, rain_s,
-                depth_out, soak_out, misfit_out,
-                water, soak, terrain, land, rain, seen, sems,
-                nat, east, west, east_r, west_r, rows_ns, W, S, G, dgc, dgr, L, R, flux, coef):
+            out[pl.ds(0, ROW_BLOCK), lanes] = ref[c].astype(jnp.int16)
+            out[pl.ds(ROW_BLOCK, 16), lanes] = jnp.zeros((16, LANES), jnp.int16)
+
+
+def decode(value, f):
+    return value.astype(jnp.float32) * (1.0 / SCALES[f])
+
+
+def same(value, *_):
+    return value
+
+
+BODY = pl.ds(HALO, CY)
+TOP = pl.ds(0, HALO)
+BOTTOM = pl.ds(HALO + CY, HALO)
+
+
+def column_halo(nat, east, west, f0, f1, fill, fix=same):
+    group = lane_ids(EXT) // COLS
+    x = jnp.full((EXT, LANES), fill, jnp.float32)
+    for f, ref, table, at in ((f1, east, FROM_EAST, 0), (f0, west, FROM_WEST, 3), (f0, east, FROM_EAST, 4), (f1, west, FROM_WEST, 7)):
+        x = jnp.where(group == at, fix(decode(rolled(ref[...], (at - table[f]) * COLS), f)), x)
+    nat[CHUNKS] = x
+
+
+def tiles(step, per=5):
+    def some(i, carry):
+        for u in range(per):
+            step(pl.multiple_of((i * per + u) * 8, 8))
+        return carry
+
+    lax.fori_loop(0, EXT // (8 * per), some, 0)
+
+
+def ring(nat, dest, copy, fix=same):
+    low = lane_ids(8) < 64
+
+    def one(at):
+        rows = pl.ds(at, 8)
+        v = [nat[c, rows, :] for c in range(CHUNKS + 1)]
+        if copy:
+            for c in range(CHUNKS):
+                dest[c, rows, :] = fix(v[c], c, rows)
+        v = [rolled(t, 64) for t in v]
+        for k in range(CHUNKS + 1):
+            dest[CHUNKS + k, rows, :] = fix(jnp.where(low, v[k - 1], v[k]), CHUNKS + k, rows)
+
+    tiles(one)
+
+
+def prepare_kernel(anc, water, soak, terrain, land, east_in, west_in, north_in, south_in,
+                   W, S, dgc, dgr, L, nat, east, west, rows_ns, G):
     f32 = jnp.float32
-    sources = (water_in, soak_in, terrain_in, land_in, rain_in, seen_in)
-    copies = [
-        pltpu.make_async_copy(src, dst, sems.at[i])
-        for i, (src, dst) in enumerate(zip(sources, (water, soak, terrain, land, rain, seen)))
-    ]
-    for copy in copies:
-        copy.start()
     slots = [anc[p] % 2 for p in range(2)]
-    lane8 = lane_ids(8)
-    lane_e = lane_ids(EXT)
-    low = lane8 < 64
-    last_lane = lane8 == LANES - 1
-    first_lane = lane8 == 0
-    body = pl.ds(HALO, CY)
-    top = pl.ds(0, HALO)
-    bottom = pl.ds(HALO + CY, HALO)
-    every = pl.ds(0, EXT)
-
     corners = pl.ds(ROW_BLOCK, 16)
-    for ref, of_rain, got, col in ((east, east_r, east_in, 0), (west, west_r, west_in, 1)):
+    for ref, got, col in ((east, east_in, 0), (west, west_in, 1)):
         lanes = pl.ds(col * LANES, LANES)
-        ref[body, :] = got[:, :].astype(jnp.int32)
-        ref[top, :] = north_in[corners, lanes].astype(jnp.int32)[16 - HALO:]
-        ref[bottom, :] = south_in[corners, lanes].astype(jnp.int32)[:HALO]
-        early = pl.ds(col * 2 * LANES, LANES)
-        late = pl.ds((col * 2 + 1) * LANES, LANES)
-        of_rain[top, :] = rain_n[pl.ds(32, 16), late].astype(jnp.int32)[16 - HALO:]
-        of_rain[bottom, :] = rain_s[pl.ds(32, 16), early].astype(jnp.int32)[:HALO]
+        ref[BODY, :] = got[:, :].astype(jnp.int32)
+        ref[TOP, :] = north_in[corners, lanes].astype(jnp.int32)[16 - HALO:]
+        ref[BOTTOM, :] = south_in[corners, lanes].astype(jnp.int32)[:HALO]
     for c in range(CHUNKS):
         lanes = pl.ds(c * LANES, LANES)
         rows_ns[0, c] = north_in[pl.ds(0, ROW_BLOCK), lanes].astype(jnp.int32)
         rows_ns[1, c] = south_in[pl.ds(0, ROW_BLOCK), lanes].astype(jnp.int32)
 
-    def decode(value, f):
-        return value.astype(f32) * (1.0 / SCALES[f])
-
-    def tile_rows(dest, f, fix=lambda v: v):
+    def tile_rows(dest, f, fix=same):
         for c in range(CHUNKS):
             lanes = pl.ds(c * LANES, LANES)
-            if f < 2:
-                dest[c, body, :] = water[slots[f], 0, :, lanes]
-            elif f < 4:
-                dest[c, body, :] = soak[slots[f - 2], 0, :, lanes]
-            elif f == 4:
-                dest[c, body, :] = terrain[0, :, lanes]
-            elif f == 5:
-                dest[c, body, :] = land[0, :, lanes].astype(f32)
-            else:
-                h = f - ROW_FIELDS
-                for d in range(CY // SHARD):
-                    dest[c, pl.ds(HALO + SHARD * d, SHARD), :] = decode(rain[d % 4, d // 4, pl.ds(SHARD * h, SHARD), lanes].astype(jnp.int32), f)
-                dest[c, top, :] = decode(rain_n[pl.ds(16 * h, 16), lanes].astype(jnp.int32)[16 - HALO:], f)
-                dest[c, bottom, :] = decode(rain_s[pl.ds(16 * h, 16), lanes].astype(jnp.int32)[:HALO], f)
-                continue
+            dest[c, BODY, :] = field_part((water, soak, terrain, land), slots, f, pl.ds(0, CY), lanes)
             put = pl.ds(HALO * f, HALO)
-            dest[c, top, :] = fix(decode(rows_ns[0, c, put, :], f))
-            dest[c, bottom, :] = fix(decode(rows_ns[1, c, put, :], f))
-
-    def column_halo(f0, f1, fill, fix=lambda v: v):
-        group = lane_e // COLS
-        x = jnp.full((EXT, LANES), fill, f32)
-        e, w = (east, west) if f0 < ROW_FIELDS else (east_r, west_r)
-        for f, ref, table, at in ((f1, e, FROM_EAST, 0), (f0, w, FROM_WEST, 3), (f0, e, FROM_EAST, 4), (f1, w, FROM_WEST, 7)):
-            x = jnp.where(group == at, fix(decode(rolled(ref[...], (at - table[f]) * COLS), f)), x)
-        nat[CHUNKS] = x
-
-    def tiles(step, per=5):
-        def some(i, carry):
-            for u in range(per):
-                step(pl.multiple_of((i * per + u) * 8, 8))
-            return carry
-
-        lax.fori_loop(0, EXT // (8 * per), some, 0)
-
-    def ring(dest, copy, fix=lambda v, c, rows: v):
-        def one(at):
-            rows = pl.ds(at, 8)
-            v = [nat[c, rows, :] for c in range(CHUNKS + 1)]
-            if copy:
-                for c in range(CHUNKS):
-                    dest[c, rows, :] = fix(v[c], c, rows)
-            v = [rolled(t, 64) for t in v]
-            for k in range(CHUNKS + 1):
-                dest[CHUNKS + k, rows, :] = fix(jnp.where(low, v[k - 1], v[k]), CHUNKS + k, rows)
-
-        tiles(one)
-
-    column_halo(0, 1, 0.0)
-    copies[0].wait()
+            dest[c, TOP, :] = fix(decode(rows_ns[0, c, put, :], f))
+            dest[c, BOTTOM, :] = fix(decode(rows_ns[1, c, put, :], f))
+
+    guard = lambda v: jnp.maximum(v, 0.1)
+    column_halo(nat, east, west, 0, 1, 0.0)
     tile_rows(W, 0)
     tile_rows(nat, 1)
-    ring(W, False)
-    guard = lambda v: jnp.maximum(v, 0.1)
-    column_halo(2, 3, 1.0, guard)
-    copies[1].wait()
+    ring(nat, W, False)
+    column_halo(nat, east, west, 2, 3, 1.0, guard)
     tile_rows(S, 2, guard)
     tile_rows(nat, 3, guard)
-    ring(S, False)
-    column_halo(4, 4, 0.0)
-    copies[2].wait()
+    ring(nat, S, False)
+    column_halo(nat, east, west, 4, 4, 0.0)
     tile_rows(nat, 4)
-    ring(G, True)
-    column_halo(5, 5, 0.0)
-    copies[3].wait()
+    ring(nat, G, True)
+    column_halo(nat, east, west, 5, 5, 0.0)
     tile_rows(nat, 5)
-    ring(L, True)
-    copies[4].wait()
-    for of_rain, col in ((east_r, 0), (west_r, 1)):
-        for d in range(CY // SHARD):
-            for half in range(2):
-                lanes = pl.ds((col * 2 + half) * LANES, LANES)
-                part = rain[d % 4, d // 4, pl.ds(2 * SHARD, 16), lanes]
-                of_rain[pl.ds(HALO + SHARD * d + 16 * half, 16), :] = part.astype(jnp.int32)
-    for h in range(HOURS):
-        column_halo(6 + h, 6 + h, 0.0)
-        tile_rows(nat, 6 + h)
-        ring(R.at[h], True, lambda v, c, rows: jnp.where(L[c, rows, :] > 0.0, v * TIME_STEP, WATER_BODY))
+    ring(nat, L, True)
     for c in range(WIDE):
-        for ref in (W, G):
-            ref[c, pl.ds(EXT, 8), :] = jnp.zeros((8, LANES), f32)
-        flux[c, pl.ds(0, 8), :] = jnp.zeros((8, LANES), f32)
+        G[c, pl.ds(EXT, 8), :] = jnp.zeros((8, LANES), f32)
+    last_lane = lane_ids(8) == LANES - 1
 
     def ground_steps(at):
         rows = pl.ds(at, 8)
@@ -248,6 +209,56 @@
             dgr[c, rows, :] = G[c, pl.ds(at + 1, 8), :] - g[c]
 
     tiles(ground_steps)
+
+
+def step_kernel(anc, owner, cond, suction, manning, prior, land_in, seen_in, rain, rain_n, rain_s, W_in, S_in, dgc, dgr, L,
+                depth_out, soak_out, misfit_out,
+                land, seen, sems, nat, east, west, W, S, R, flux, coef):
+    f32 = jnp.float32
+    copies = [
+        pltpu.make_async_copy(src, dst, sems.at[i])
+        for i, (src, dst) in enumerate(((land_in, land), (seen_in, seen)))
+    ]
+    for copy in copies:
+        copy.start()
+    slots = [anc[p] % 2 for p in range(2)]
+    lane8 = lane_ids(8)
+    low = lane8 < 64
+    last_lane = lane8 == LANES - 1
+    first_lane = lane8 == 0
+
+    for ref, col in ((east, 0), (west, 1)):
+        for d in range(CY // SHARD):
+            for half in range(2):
+                lanes = pl.ds((col * 2 + half) * LANES, LANES)
+                part = rain[d % 4, d // 4, pl.ds(2 * SHARD, 16), lanes]
+                ref[pl.ds(HALO + SHARD * d + 16 * half, 16), :] = part.astype(jnp.int32)
+        early = pl.ds(col * 2 * LANES, LANES)
+        late = pl.ds((col * 2 + 1) * LANES, LANES)
+        ref[TOP, :] = rain_n[pl.ds(32, 16), late].astype(jnp.int32)[16 - HALO:]
+        ref[BOTTOM, :] = rain_s[pl.ds(32, 16), early].astype(jnp.int32)[:HALO]
+    for h in range(HOURS):
+        f = ROW_FIELDS + h
+        column_halo(nat, east, west, f, f, 0.0)
+        for c in range(CHUNKS):
+            lanes = pl.ds(c * LANES, LANES)
+            for d in range(CY // SHARD):
+                part = rain[d % 4, d // 4, pl.ds(SHARD * h, SHARD), lanes]
+                nat[c, pl.ds(HALO + SHARD * d, SHARD), :] = decode(part.astype(jnp.int32), f)
+            nat[c, TOP, :] = decode(rain_n[pl.ds(16 * h, 16), lanes].astype(jnp.int32)[16 - HALO:], f)
+            nat[c, BOTTOM, :] = decode(rain_s[pl.ds(16 * h, 16), lanes].astype(jnp.int32)[:HALO], f)
+        ring(nat, R.at[h], True, lambda v, c, rows: jnp.where(L[c, rows, :] > 0.0, v * TIME_STEP, WATER_BODY))
+    for c in range(WIDE):
+        W[c, pl.ds(EXT, 8), :] = jnp.zeros((8, LANES), f32)
+        flux[c, pl.ds(0, 8), :] = jnp.zeros((8, LANES), f32)
+
+    def copy_in(at):
+        rows = pl.ds(at, 8)
+        for c in range(WIDE):
+            W[c, rows, :] = W_in[c, rows, :]
+            S[c, rows, :] = S_in[c, rows, :]
+
+    tiles(copy_in)
 
     for k in range(3):
         pair = []
@@ -320,7 +331,8 @@
 
         return lax.fori_loop(0, CY // 16, score, total)
 
-    copies[5].wait()
+    for copy in copies:
+        copy.wait()
     zero = jnp.zeros((8, LANES), f32)
     one, two, cells = lax.fori_loop(0, HOURS, hour, (zero, zero, zero))
 
@@ -372,7 +384,7 @@
 
 
 def pack_rows(anc, fields):
-    shape = (ROW_BLOCK, CX)
+    shape = (ROW_BLOCK + 16, CX)
     return pl.pallas_call(
         rows_kernel,
         out_shape=[jax.ShapeDtypeStruct(shape, jnp.int16)] * 2,
@@ -384,10 +396,29 @@
     )(anc, *fields, *fields)
 
 
+def prepare(*args):
+    wide = (WIDE, EXT, LANES)
+    return pl.pallas_call(
+        prepare_kernel,
+        out_shape=[jax.ShapeDtypeStruct(wide, jnp.float32)] * 5,
+        in_specs=[SM] + [VM] * 8,
+        out_specs=[VM] * 5,
+        scratch_shapes=[
+            pltpu.VMEM((CHUNKS + 1, EXT, LANES), jnp.float32),
+            pltpu.VMEM((EXT, LANES), jnp.int32),
+            pltpu.VMEM((EXT, LANES), jnp.int32),
+            pltpu.VMEM((2, CHUNKS, ROW_BLOCK, LANES), jnp.int32),
+            pltpu.VMEM((WIDE, EXT + 8, LANES), jnp.float32),
+        ],
+        compiler_params=pltpu.CompilerParams(vmem_limit_bytes=20 << 20),
+        name="prepare",
+    )(*args)
+
+
 def steps(*args):
     f32 = jnp.float32
-    wide = pltpu.VMEM((WIDE, EXT, LANES), f32)
     tall = pltpu.VMEM((WIDE, EXT + 8, LANES), f32)
+    land, seen = args[6:8]
     return pl.pallas_call(
         step_kernel,
         out_shape=(
@@ -395,25 +426,50 @@
             jax.ShapeDtypeStruct((2, 1, CY, CX), f32),
             jax.ShapeDtypeStruct((1, LANES), f32),
         ),
-        in_specs=[SM] * 6 + [pl.BlockSpec(memory_space=pltpu.HBM)] * 6 + [VM] * 6,
+        in_specs=[SM] * 6 + [pl.BlockSpec(memory_space=pltpu.HBM)] * 2 + [VM] * 8,
         out_specs=(VM,) * 3,
-        scratch_shapes=[pltpu.VMEM(x.shape, x.dtype) for x in args[6:12]]
-        + [
-            pltpu.SemaphoreType.DMA((6,)),
+        scratch_shapes=[
+            pltpu.VMEM(land.shape, land.dtype),
+            pltpu.VMEM(seen.shape, seen.dtype),
+            pltpu.SemaphoreType.DMA((2,)),
             pltpu.VMEM((CHUNKS + 1, EXT, LANES), f32),
             pltpu.VMEM((EXT, LANES), jnp.int32),
             pltpu.VMEM((EXT, LANES), jnp.int32),
-            pltpu.VMEM((EXT, LANES), jnp.int32),
-            pltpu.VMEM((EXT, LANES), jnp.int32),
-            pltpu.VMEM((2, CHUNKS, ROW_BLOCK, LANES), jnp.int32),
-            tall, wide, tall, wide, wide, wide,
+            tall,
+            pltpu.VMEM((WIDE, EXT, LANES), f32),
             pltpu.VMEM((HOURS, WIDE, EXT, LANES), f32),
             tall,
             pltpu.VMEM((3, WIDE, 8, LANES), f32),
         ],
-        compiler_params=pltpu.CompilerParams(vmem_limit_bytes=40 << 20),
+        compiler_params=pltpu.CompilerParams(vmem_limit_bytes=24 << 20),
         name="steps",
     )(*args)
+
+
+def weigh_kernel(group, lines, out):
+    groups = lines.shape[1]
+    table = lines[0]
+    for i in range(1, lines.shape[0]):
+        table = table + lines[i]
+    lane = lane_ids(groups)
+    pick = lambda values, at: jnp.sum(jnp.where(lane == at, values, 0.0), axis=1, keepdims=True)
+    mean = 0.5 * pick(lines[0], 3)
+    raw = mean * jnp.exp(-SHARPNESS * table / pick(table, 2))
+    raw = jnp.where(lane < 2, raw, 0.0)
+    weights = raw / jnp.sum(raw)
+    mine = lax.broadcasted_iota(jnp.int32, (groups, LANES), 0) == group[0]
+    for p in range(2):
+        out[p] = jnp.sum(jnp.where(mine & (lane == p), weights, 0.0))
+
+
+def weigh(group, lines):
+    return pl.pallas_call(
+        weigh_kernel,
+        out_shape=jax.ShapeDtypeStruct((2,), jnp.float32),
+        in_specs=[SM, VM],
+        out_specs=SM,
+        name="weigh",
+    )(group, lines)
 
 
 def route(down, right):
@@ -442,7 +498,7 @@
 
     def with_corners(block, rows):
         corner = jnp.concatenate([from_east[rows], from_west[rows]] * 2, axis=1)
-        return jnp.concatenate([block, corner], axis=0)
+        return lax.dynamic_update_slice(block, corner, (ROW_BLOCK, 0))
 
     from_south = lax.ppermute(with_corners(to_north, slice(0, 16)), "space", route(-1, 0))
     from_north = lax.ppermute(with_corners(to_south, slice(CY - 16, CY)), "space", route(1, 0))
@@ -454,20 +510,15 @@
     a, b = rain[0, 0], rain[-1, -1]
     rain_south = lax.ppermute(jnp.concatenate([a[0:16], a[32:48], a[64:80]], axis=0), "space", route(-1, 0))
     rain_north = lax.ppermute(jnp.concatenate([b[16:32], b[48:64], b[64:80]], axis=0), "space", route(1, 0))
-
-    depth, wet, score = steps(anc, owner, cond, suction, manning, prior, water, soak, terrain, land, rain, seen,
-                              from_east, from_west, from_north, from_south, rain_north, rain_south)
+    ready = prepare(anc, *fields, from_east, from_west, from_north, from_south)
+    depth, wet, score = steps(anc, owner, cond, suction, manning, prior, land, seen, rain, rain_north, rain_south, *ready)
 
     score = score + lax.ppermute(score, "space", [(i, i ^ 1) for i in range(tiles)])
     peers = [[t * groups + d for t in range(k, tiles, 2) for d in range(groups)] for k in range(2)]
-    line = jnp.broadcast_to(score[None], (tiles // 2 * groups, 1, LANES))
-    line = lax.all_to_all(line, ("space", "dom"), 0, 0, axis_index_groups=peers, tiled=True)
-    line = line.reshape(tiles // 2, groups, LANES)
-    table = jnp.sum(line, axis=0)
-    raw = 0.5 * line[0, :, 3:4] * jnp.exp(-SHARPNESS * table[:, :2] / table[:, 2:3])
-    weights = raw / jnp.sum(raw)
-    mine = lax.broadcasted_iota(jnp.int32, (groups, 1), 0) == lax.axis_index("dom")
-    return depth, wet, jnp.sum(jnp.where(mine, weights, 0.0), axis=0)
+    lines = jnp.broadcast_to(score[None], (tiles // 2 * groups, 1, LANES))
+    lines = lax.all_to_all(lines, ("space", "dom"), 0, 0, axis_index_groups=peers, tiled=True)
+    weights = weigh(lax.axis_index("dom")[None], lines.reshape(tiles // 2, groups, LANES))
+    return depth, wet, weights
 
 
 def solution(mesh):

time: 124 us -> 118 us (0.952)
  blocking collectives: 0 us -> 25.8 us
  waiting for transfers between devices: 19.9 us -> 5 us
  starting transfers between devices: 46.7 us -> 32.1 us
  other arithmetic: 6.12 us -> 2.95 us
  Pallas kernels: 45.8 us -> 48.4 us
  local copies, waits for them, and re-layouts: 3.66 us -> 1.82 us
    all_to_all x0 -> x1, blocking collectives: none -> 25.8 us  [window(): lax.all_to_all(lines, ('space', 'dom'), 0, 0, axis_index_groups=peers, ti...]
    all_to_all x1 -> x0, starting transfers between devices: 14.7 us -> none  [window(): lax.all_to_all(line, ('space', 'dom'), 0, 0, axis_index_groups=peers, til...]
    all_to_all x1 -> x0, waiting for transfers between devices: 10.1 us -> none  [window(): lax.all_to_all(line, ('space', 'dom'), 0, 0, axis_index_groups=peers, til...]
    pallas_call x0 -> x2, Pallas kernels: none -> 6.46 us  [the longest x1 4.76 us: prepare(): pl.pallas_call(prepare_kernel, out_shape=[jax.ShapeDtypeStruct(wide, jnp....]
    ppermute x1, waiting for transfers between devices: 5.01 us -> 0.19 us  [window(): lax.ppermute(jnp.concatenate([a[0:16], a[32:48], a[64:80]], axis=0), 'spa...]
    pallas_call x1, Pallas kernels: 40.7 us -> 36.8 us  [steps(): pl.pallas_call(step_kernel, out_shape=(jax.ShapeDtypeStruct((2, 1, CY, CX...]
    concatenate x2 -> x0, other arithmetic: 3.14 us -> none  [with_corners(): return jnp.concatenate([block, corner], axis=0)]
    reduce_sum x3 -> x0, other arithmetic: 1.81 us -> none  [the longest x1 1.14 us: window(): return (depth, wet, jnp.sum(jnp.where(mine, weights, 0.0), axis=0))]
  transfers between devices with their start and end apart: 10 -> 9, of which waited for: 6 -> 5; matrix products, arithmetic and copies ran while one was open for 3% -> 2% of each run, Pallas kernels for 2% -> 6%
where the time goes in v1:
time: 118 us; the launch traced here: 117 us
  Pallas kernels  48.4 us (41%)
  starting transfers between devices  32.1 us (27%)
  blocking collectives  25.8 us (22%)
  waiting for transfers between devices  5 us (4%)
  other arithmetic  2.95 us (2%)
  local copies, waits for them, and re-layouts  1.82 us (2%)
    pallas_call x1, Pallas kernels, steps(): pl.pallas_call(step_kernel, out_shape=(jax.ShapeDtypeStruct((2, 1, CY, CX...  36.8 us
    all_to_all x1, blocking collectives, window(): lax.all_to_all(lines, ('space', 'dom'), 0, 0, axis_index_groups=peers, ti...  25.8 us
    ppermute x1, starting transfers between devices, window(): lax.ppermute(shard, 'dom', [(i, (i + line) % groups) for i in range(group...  6.61 us
    ppermute x1, starting transfers between devices, window(): lax.ppermute(jnp.concatenate([b[16:32], b[48:64], b[64:80]], axis=0), 'sp...  5.49 us
    ppermute x1, starting transfers between devices, window(): lax.ppermute(with_corners(to_south, slice(CY - 16, CY)), 'space', route(1...  5.48 us
    pallas_call x1, Pallas kernels, prepare(): pl.pallas_call(prepare_kernel, out_shape=[jax.ShapeDtypeStruct(wide, jnp....  4.76 us
    ppermute x1, starting transfers between devices, window(): lax.ppermute(score, 'space', [(i, i ^ 1) for i in range(tiles)])  4.42 us
    all_to_all x1, starting transfers between devices, window(): lax.all_to_all(jnp.broadcast_to(pair[None], (line,) + pair.shape), 'dom',...  4.17 us
  transfers between devices with their start and end apart: 9, of which 5 were waited for; matrix products, arithmetic and copies ran while one was open for 2% of the time, Pallas kernels for 6%

profile of v1, /device:TPU:1, one launch (start us, length us, event | category | flops | bytes accessed | tf_op | source)
XLA Modules:
  0.0 117.0 jit_solution(6610639173225901171)
XLA Ops:
  0.6 3.2 %pack_columns.1 = (s16[256,128]{1,0:T(8,128)(2,1)}, s16[256,128]{1,0:T(8,128)(2,1)}, s16[2,32,512]{2,1,0:T(8,128)(2,1)}) custom-call(s32[2]{0:T(128)} %anc.7, f32[2,1,256,512]{3,2,1,0:T(8,128)} %water.1, f32[2,1,256,512]{3,2,1,0:T(8,128)} %soak.1, f32[1,256,512]{2,1,0:T(8,128)} %terrain.1, s32[1,256,512]{2,1,0:T(8,128)} %land_in.1, ...), custom_call_target="tpu_custom_call" | custom-call | tf_op jit(solution)/shard_map/pack_columns/pallas_call | solution.py:376
  3.8 3.2 %collective-permute-start = (s16[256,128]{1,0:T(8,128)(2,1)}, s16[256,128]{1,0:T(8,128)(2,1)S(1)}, u32[]{:S(2)}, u32[]{:S(2)}) collective-permute-start(s16[256,128]{1,0:T(8,128)(2,1)} %get-tuple-element.17), channel_id=1, source_target_pairs={{0,24},{8,0},{16,8},{24,16},{32,56},{40,32},{48,40},{56,48},{64,88... | collective-permute-start | bytes 196616 | tf_op jit(solution)/shard_map/ppermute | solution.py:490
  7.0 0.0 collective-permute-start.1
  7.1 1.6 %collective-permute-done.east_in = s16[256,128]{1,0:T(8,128)(2,1)S(1)} collective-permute-done((s16[256,128]{1,0:T(8,128)(2,1)}, s16[256,128]{1,0:T(8,128)(2,1)S(1)}, u32[]{:S(2)}, u32[]{:S(2)}) %collective-permute-start) | collective-permute-done | bytes 65568 | tf_op jit(solution)/shard_map/ppermute | solution.py:490
  8.7 0.4 collective-permute-done.1.west_in
  9.1 0.8 add_add_fusion
  9.9 6.6 %collective-permute-start.2 = (s16[80,512]{1,0:T(8,128)(2,1)S(1)}, s16[80,512]{1,0:T(8,128)(2,1)S(1)}, u32[]{:S(2)}, u32[]{:S(2)}) collective-permute-start(s16[80,512]{1,0:T(8,128)(2,1)S(1)} %add_add_fusion), channel_id=1, source_target_pairs={{0,4},{1,5},{2,6},{3,7},{4,0},{5,1},{6,2},{7,3},{8,12},{9,13},{10,... | collective-permute-start | bytes 245768 | tf_op jit(solution)/shard_map/ppermute | solution.py:497
  16.6 1.9 %collective-permute-done.2 = s16[80,512]{1,0:T(8,128)(2,1)S(1)} collective-permute-done((s16[80,512]{1,0:T(8,128)(2,1)S(1)}, s16[80,512]{1,0:T(8,128)(2,1)S(1)}, u32[]{:S(2)}, u32[]{:S(2)}) %collective-permute-start.2) | collective-permute-done | bytes 81952 | tf_op jit(solution)/shard_map/ppermute | solution.py:497
  18.5 0.9 select_bitcast_fusion.1
  19.4 0.9 broadcast_in_dim.8
  20.3 4.2 %all-to-all-start = ((s16[4,2,80,512]{3,2,1,0:T(8,128)(2,1)}), s16[4,2,80,512]{3,2,1,0:T(8,128)(2,1)}, u32[]{:S(2)}, u32[]{:S(2)}) async-start(s16[4,2,80,512]{3,2,1,0:T(8,128)(2,1)} %broadcast_in_dim.8), calls=%async_computation | async-start | bytes 1310720 | tf_op jit(solution)/shard_map/all_to_all | solution.py:508
  24.5 0.0 copy-start
  24.5 0.0 copy-start.1
  24.5 0.0 copy-start.2
  24.5 0.0 copy-start.3
  24.5 0.0 copy-start.5
  24.5 1.9 %pack_rows.1 = (s16[96,512]{1,0:T(8,128)(2,1)}, s16[96,512]{1,0:T(8,128)(2,1)}) custom-call(s32[2]{0:T(128)} %anc.7, f32[2,1,256,512]{3,2,1,0:T(8,128)} %water.1, f32[2,1,256,512]{3,2,1,0:T(8,128)} %soak.1, f32[1,256,512]{2,1,0:T(8,128)} %terrain.1, s32[1,256,512]{2,1,0:T(8,128)} %land_in.1, f32[2,1,256,512]{3,2,1,0:T(8,128)} %water.1, ...), custom_call_target="tpu_custom_call" | custom-call | tf_op jit(solution)/shard_map/pack_rows/pallas_call | solution.py:388
  26.4 0.6 add_dynamic-update-slice_fusion.1
  27.1 1.3 %collective-permute-start.6 = (s16[96,512]{1,0:T(8,128)(2,1)}, s16[96,512]{1,0:T(8,128)(2,1)S(1)}, u32[]{:S(2)}, u32[]{:S(2)}) collective-permute-start(s16[96,512]{1,0:T(8,128)(2,1)} %add_dynamic-update-slice_fusion.1), channel_id=1, source_target_pairs={{32,0},{40,8},{48,16},{56,24},{64,32},{72,40},{80,48},{88,56},{96,... | collective-permute-start | bytes 294920 | tf_op jit(solution)/shard_map/ppermute | solution.py:503
  28.3 0.6 add_dynamic-update-slice_fusion
  28.9 5.5 %collective-permute-start.5 = (s16[96,512]{1,0:T(8,128)(2,1)}, s16[96,512]{1,0:T(8,128)(2,1)S(1)}, u32[]{:S(2)}, u32[]{:S(2)}) collective-permute-start(s16[96,512]{1,0:T(8,128)(2,1)} %add_dynamic-update-slice_fusion), channel_id=1, source_target_pairs={{0,32},{8,40},{16,48},{24,56},{32,64},{40,72},{48,80},{56,88},{64,... | collective-permute-start | bytes 294920 | tf_op jit(solution)/shard_map/ppermute | solution.py:504
  34.4 0.0 all-to-all-done.rain
  34.4 0.8 slice_bitcast_fusion.2
  35.3 5.5 %collective-permute-start.3 = (s16[48,512]{1,0:T(8,128)(2,1)S(1)}, s16[48,512]{1,0:T(8,128)(2,1)S(1)}, u32[]{:S(2)}, u32[]{:S(2)}) collective-permute-start(s16[48,512]{1,0:T(8,128)(2,1)S(1)} %pad_add_fusion.1), channel_id=1, source_target_pairs={{0,32},{8,40},{16,48},{24,56},{32,64},{40,72},{48,80},{56,88},{64,... | collective-permute-start | bytes 147464 | tf_op jit(solution)/shard_map/ppermute | solution.py:512
  40.8 0.0 copy-start.4
  40.8 0.0 copy-start.6
  40.8 0.0 copy-start.7
  40.8 0.0 copy-start.8
  40.8 0.0 copy-start.9
  40.8 0.0 copy-start.10
  40.9 1.4 %collective-permute-start.4 = (s16[48,512]{1,0:T(8,128)(2,1)S(1)}, s16[48,512]{1,0:T(8,128)(2,1)S(1)}, u32[]{:S(2)}, u32[]{:S(2)}) collective-permute-start(s16[48,512]{1,0:T(8,128)(2,1)S(1)} %pad_add_fusion.2), channel_id=1, source_target_pairs={{32,0},{40,8},{48,16},{56,24},{64,32},{72,40},{80,48},{88,56},{96,... | collective-permute-start | bytes 147464 | tf_op jit(solution)/shard_map/ppermute | solution.py:511
  42.3 0.0 collective-permute-done.6.south_in
  42.3 0.0 collective-permute-done.5.north_in
  42.3 0.0 copy-done
  42.3 0.0 copy-done.1
  42.3 0.0 copy-done.2
  42.3 0.0 copy-done.3
  42.3 0.0 copy-done.5
  42.4 4.8 %prepare.1 = (f32[9,280,128]{2,1,0:T(8,128)S(1)}, f32[9,280,128]{2,1,0:T(8,128)S(1)}, f32[9,280,128]{2,1,0:T(8,128)S(1)}, f32[9,280,128]{2,1,0:T(8,128)S(1)}, f32[9,280,128]{2,1,0:T(8,128)S(1)}) custom-call(s32[2]{0:T(128)S(1)} %copy-done.5, f32[2,1,256,512]{3,2,1,0:T(8,128)S(1)} %copy-done, f32[2,1,256,512]{3,2,1,0:T(8,128)S(1)} %copy-done.1, ...), custom_call_target="tpu_custom_call" | custom-call | tf_op jit(solution)/shard_map/prepare/pallas_call | solution.py:401
  47.1 0.0 collective-permute-done.3.rain_n
  47.1 0.2 collective-permute-done.4.rain_s
  47.3 0.0 copy-done.8
  47.3 0.0 copy-done.9
  47.4 36.8 %steps.1 = (f32[2,1,256,512]{3,2,1,0:T(8,128)}, f32[2,1,256,512]{3,2,1,0:T(8,128)}, f32[1,128]{1,0:T(1,128)S(1)}) custom-call(s32[2]{0:T(128)S(1)} %copy-done.5, s32[2]{0:T(128)S(1)} %copy-done.6, f32[16]{0:T(128)S(1)} %copy-done.7, f32[16]{0:T(128)S(1)} %copy-done.8, f32[16]{0:T(128)S(1)} %copy-done.9, f32[2]{0:T(128)S(1)} %copy-done.10, ...), custom_call_target="tpu_custom_call" | custom-call | tf_op jit(solution)/shard_map/steps/pallas_call | solution.py:422
  84.1 4.4 %collective-permute-start.7 = (f32[1,128]{1,0:T(1,128)S(1)}, f32[1,128]{1,0:T(1,128)S(1)}, u32[]{:S(2)}, u32[]{:S(2)}) collective-permute-start(f32[1,128]{1,0:T(1,128)S(1)} %get-tuple-element.28), channel_id=1, source_target_pairs={{0,8},{8,0},{16,24},{24,16},{32,40},{40,32},{48,56},{56,48},{64,72... | collective-permute-start | bytes 1544 | tf_op jit(solution)/shard_map/ppermute | solution.py:516
  88.6 0.8 collective-permute-done.7
  89.4 25.8 %all_to_all.10 = f32[128,1,128]{2,1,0:T(1,128)} all-to-all(f32[128,1,128]{2,1,0:T(1,128)S(1)} %broadcast_in_dim.20), channel_id=1, replica_groups={{0,1,2,3,4,5,6,7,16,17,18,19,20,21,22,23,32,33,34,35,36,37,38,39,48,49,..., dimensions={0} | all-to-all | bytes 131072 | tf_op jit(solution)/shard_map/all_to_all | solution.py:519
  115.3 1.7 %weigh.1 = f32[2]{0:T(128)} custom-call(s32[1]{0:T(128)} %bitcast.9.group, f32[16,8,128]{2,1,0:T(8,128)} %bitcast.23), custom_call_target="tpu_custom_call" | custom-call | tf_op jit(solution)/shard_map/weigh/pallas_call | solution.py:466
  (11 shorter events, 0.1 us)
Async XLA Ops:
  3.8 4.8 %collective-permute-start = (s16[256,128]{1,0:T(8,128)(2,1)}, s16[256,128]{1,0:T(8,128)(2,1)S(1)}, u32[]{:S(2)}, u32[]{:S(2)}) collective-permute-start(s16[256,128]{1,0:T(8,128)(2,1)} %get-tuple-element.17), channel_id=1, source_target_pairs={{0,24},{8,0},{16,8},{24,16},{32,56},{40,32},{48,40},{56,48},{64,88... | collective-permute-start | bytes 196616 | tf_op jit(solution)/shard_map/ppermute | solution.py:490
  7.0 2.1 %collective-permute-start.1 = (s16[256,128]{1,0:T(8,128)(2,1)}, s16[256,128]{1,0:T(8,128)(2,1)S(1)}, u32[]{:S(2)}, u32[]{:S(2)}) collective-permute-start(s16[256,128]{1,0:T(8,128)(2,1)} %get-tuple-element.18), channel_id=1, source_target_pairs={{0,8},{8,16},{16,24},{24,0},{32,40},{40,48},{48,56},{56,32},{64,72... | collective-permute-start | bytes 196616 | tf_op jit(solution)/shard_map/ppermute | solution.py:491
  9.9 8.5 %collective-permute-start.2 = (s16[80,512]{1,0:T(8,128)(2,1)S(1)}, s16[80,512]{1,0:T(8,128)(2,1)S(1)}, u32[]{:S(2)}, u32[]{:S(2)}) collective-permute-start(s16[80,512]{1,0:T(8,128)(2,1)S(1)} %add_add_fusion), channel_id=1, source_target_pairs={{0,4},{1,5},{2,6},{3,7},{4,0},{5,1},{6,2},{7,3},{8,12},{9,13},{10,... | collective-permute-start | bytes 245768 | tf_op jit(solution)/shard_map/ppermute | solution.py:497
  20.3 14.2 %all-to-all-start = ((s16[4,2,80,512]{3,2,1,0:T(8,128)(2,1)}), s16[4,2,80,512]{3,2,1,0:T(8,128)(2,1)}, u32[]{:S(2)}, u32[]{:S(2)}) async-start(s16[4,2,80,512]{3,2,1,0:T(8,128)(2,1)} %broadcast_in_dim.8), calls=%async_computation | async-start | bytes 1310720 | tf_op jit(solution)/shard_map/all_to_all | solution.py:508
  24.5 17.8 %copy-start = (f32[2,1,256,512]{3,2,1,0:T(8,128)S(1)}, f32[2,1,256,512]{3,2,1,0:T(8,128)}, u32[]{:S(2)}) copy-start(f32[2,1,256,512]{3,2,1,0:T(8,128)} %water.1) | copy-start | bytes 3145732
  24.5 17.8 %copy-start.1 = (f32[2,1,256,512]{3,2,1,0:T(8,128)S(1)}, f32[2,1,256,512]{3,2,1,0:T(8,128)}, u32[]{:S(2)}) copy-start(f32[2,1,256,512]{3,2,1,0:T(8,128)} %soak.1) | copy-start | bytes 3145732
  24.5 17.8 %copy-start.2 = (s32[1,256,512]{2,1,0:T(8,128)S(1)}, s32[1,256,512]{2,1,0:T(8,128)}, u32[]{:S(2)}) copy-start(s32[1,256,512]{2,1,0:T(8,128)} %land_in.1) | copy-start | bytes 1572868
  24.5 17.8 %copy-start.3 = (f32[1,256,512]{2,1,0:T(8,128)S(1)}, f32[1,256,512]{2,1,0:T(8,128)}, u32[]{:S(2)}) copy-start(f32[1,256,512]{2,1,0:T(8,128)} %terrain.1) | copy-start | bytes 1572868
  24.5 17.8 %copy-start.5 = (s32[2]{0:T(128)S(1)}, s32[2]{0:T(128)}, u32[]{:S(2)}) copy-start(s32[2]{0:T(128)} %anc.7) | copy-start | bytes 28
  27.1 15.2 %collective-permute-start.6 = (s16[96,512]{1,0:T(8,128)(2,1)}, s16[96,512]{1,0:T(8,128)(2,1)S(1)}, u32[]{:S(2)}, u32[]{:S(2)}) collective-permute-start(s16[96,512]{1,0:T(8,128)(2,1)} %add_dynamic-update-slice_fusion.1), channel_id=1, source_target_pairs={{32,0},{40,8},{48,16},{56,24},{64,32},{72,40},{80,48},{88,56},{96,... | collective-permute-start | bytes 294920 | tf_op jit(solution)/shard_map/ppermute | solution.py:503
  28.9 13.4 %collective-permute-start.5 = (s16[96,512]{1,0:T(8,128)(2,1)}, s16[96,512]{1,0:T(8,128)(2,1)S(1)}, u32[]{:S(2)}, u32[]{:S(2)}) collective-permute-start(s16[96,512]{1,0:T(8,128)(2,1)} %add_dynamic-update-slice_fusion), channel_id=1, source_target_pairs={{0,32},{8,40},{16,48},{24,56},{32,64},{40,72},{48,80},{56,88},{64,... | collective-permute-start | bytes 294920 | tf_op jit(solution)/shard_map/ppermute | solution.py:504
  35.3 11.9 %collective-permute-start.3 = (s16[48,512]{1,0:T(8,128)(2,1)S(1)}, s16[48,512]{1,0:T(8,128)(2,1)S(1)}, u32[]{:S(2)}, u32[]{:S(2)}) collective-permute-start(s16[48,512]{1,0:T(8,128)(2,1)S(1)} %pad_add_fusion.1), channel_id=1, source_target_pairs={{0,32},{8,40},{16,48},{24,56},{32,64},{40,72},{48,80},{56,88},{64,... | collective-permute-start | bytes 147464 | tf_op jit(solution)/shard_map/ppermute | solution.py:512
  40.8 6.5 %copy-start.4 = (bf16[2,1,256,512]{3,2,1,0:T(8,128)(2,1)S(1)}, bf16[2,1,256,512]{3,2,1,0:T(8,128)(2,1)}, u32[]{:S(2)}) copy-start(bf16[2,1,256,512]{3,2,1,0:T(8,128)(2,1)} %seen_in.1) | copy-start | bytes 1572868
  40.8 6.5 %copy-start.6 = (s32[2]{0:T(128)S(1)}, s32[2]{0:T(128)}, u32[]{:S(2)}) copy-start(s32[2]{0:T(128)} %owner.1) | copy-start | bytes 28
  40.8 6.5 %copy-start.7 = (f32[16]{0:T(128)S(1)}, f32[16]{0:T(128)}, u32[]{:S(2)}) copy-start(f32[16]{0:T(128)} %cond.1) | copy-start | bytes 196
  40.8 6.5 %copy-start.8 = (f32[16]{0:T(128)S(1)}, f32[16]{0:T(128)}, u32[]{:S(2)}) copy-start(f32[16]{0:T(128)} %suction.1) | copy-start | bytes 196
  40.8 6.5 %copy-start.9 = (f32[16]{0:T(128)S(1)}, f32[16]{0:T(128)}, u32[]{:S(2)}) copy-start(f32[16]{0:T(128)} %manning.1) | copy-start | bytes 196
  40.8 6.5 %copy-start.10 = (f32[2]{0:T(128)S(1)}, f32[2]{0:T(128)}, u32[]{:S(2)}) copy-start(f32[2]{0:T(128)} %prior.1) | copy-start | bytes 28
  40.9 6.5 %collective-permute-start.4 = (s16[48,512]{1,0:T(8,128)(2,1)S(1)}, s16[48,512]{1,0:T(8,128)(2,1)S(1)}, u32[]{:S(2)}, u32[]{:S(2)}) collective-permute-start(s16[48,512]{1,0:T(8,128)(2,1)S(1)} %pad_add_fusion.2), channel_id=1, source_target_pairs={{32,0},{40,8},{48,16},{56,24},{64,32},{72,40},{80,48},{88,56},{96,... | collective-permute-start | bytes 147464 | tf_op jit(solution)/shard_map/ppermute | solution.py:511
  84.1 5.2 %collective-permute-start.7 = (f32[1,128]{1,0:T(1,128)S(1)}, f32[1,128]{1,0:T(1,128)S(1)}, u32[]{:S(2)}, u32[]{:S(2)}) collective-permute-start(f32[1,128]{1,0:T(1,128)S(1)} %get-tuple-element.28), channel_id=1, source_target_pairs={{0,8},{8,0},{16,24},{24,16},{32,40},{40,32},{48,56},{56,48},{64,72... | collective-permute-start | bytes 1544 | tf_op jit(solution)/shard_map/ppermute | solution.py:516
